TPU v7x, 32 devices: a whole 2x2x4 slice. The times are simulated.
32 devices in a mesh: group: 2 (over x), tile: 16 (over z, y, core).
Axes of the slice: x: 2, y: 2, z: 4, core: 2. Of those that a mesh axis runs over, the one named last changes fastest.
Arguments:
- latents: bfloat16 [384, 16, 128], P(('group', 'tile')), parts along dimension 0, may hold values from -6 to 6
- clip_index: int32 [8], P('group'), parts along dimension 0, may hold values from 0 to 1, never falling along the last dimension, each value on 1 to 3 neighbouring positions
- first_conv: bfloat16 [3, 3, 3, 16, 384], replicated, may hold values from -0.3125 to 0.3125
- first_gain: float32 [384], replicated, may hold values from 0.4 to 1.6
- middle_conv: bfloat16 [3, 3, 3, 384, 384], replicated, may hold values from -0.0625 to 0.0625
- head_gain: float32 [384], replicated, may hold values from 0.4 to 1.6
- head_weight: bfloat16 [384, 48], replicated, may hold values from -0.3125 to 0.3125
Outputs:
- pixels: float32 [32, 2, 3, 48, 128], P(('group', 'tile')), parts along dimension 0
There are 2 independent parts, one for each index of `group`. A program takes and returns all parts, laid end to end along the dimension named above; an argument that names none is the same for every part. Nothing has to cross between parts.
Inputs may be any that keep to these rules, and one draw needn't show every extreme that they name: `clip_index`: clip numbers never fall along the frames; each clip holds 1 to 3 consecutive frames.
All inputs are finite; a program needn't handle non-finite values.
Results may differ from a plain program's by a relative error of at most 0.01.
Values may be sent and summed in bfloat16 or wider, within the bound.
A program may use at most 128 MiB of HBM per device.

v0:
```python
import jax
import jax.numpy as jnp
from jax import lax
from jax.sharding import PartitionSpec as P

CLAT = 16
CH = 384
PATCH = 16
STRIPS = 8
TF = 2
WS = 16
HL = 48


def shifted(value, axis, by):
    length = lax.axis_size(axis)
    return lax.ppermute(value, axis, [(i, (i + by) % length) for i in range(length)])


def partner(value, axis, apart):
    return lax.ppermute(value, axis, [(i, i ^ 1 << apart) for i in range(lax.axis_size(axis))])


def norm_act(values, gain):
    scale = lax.rsqrt(jnp.mean(values * values, axis=-1, keepdims=True) + 1e-06)
    return jax.nn.silu(values * scale * gain)


def extend(field, column, older):
    left = shifted(field[:, :, -1:], "tile", 1)
    left = jnp.where(column > 0, left, jnp.zeros_like(left))
    right = shifted(field[:, :, :1], "tile", -1)
    right = jnp.where(column < STRIPS - 1, right, jnp.zeros_like(right))
    wide = jnp.concatenate([left, field, right], axis=2)
    cache = shifted(field, "tile", STRIPS)
    corner_left = shifted(field[-2:, :, -1:], "tile", STRIPS + 1)
    corner_left = jnp.where(column > 0, corner_left, jnp.zeros_like(corner_left))
    corner_right = shifted(field[-2:, :, :1], "tile", STRIPS - 1)
    corner_right = jnp.where(column < STRIPS - 1, corner_right, jnp.zeros_like(corner_right))
    older = jnp.concatenate([corner_left, cache, corner_right], axis=2)
    return jnp.concatenate([older, wide], axis=0)


def causal_conv(full, keep, weight):
    frames = full.shape[0] - 2
    height = full.shape[1]
    width = full.shape[2] - 2
    channels = full.shape[3]
    outs = weight.shape[-1]
    padded = jnp.pad(full, ((0, 0), (1, 1), (0, 0), (0, 0)))
    total = jnp.zeros((frames * height * width, outs), jnp.float32)
    for step_t in range(3):
        slab = (
            padded[step_t : step_t + frames]
            * keep[:, step_t].astype(full.dtype)[:, None, None, None]
        )
        for step_r in range(3):
            rows = slab[:, step_r : step_r + height]
            stacked = jnp.concatenate(
                [rows[:, :, step_c : step_c + width] for step_c in range(3)], axis=-1
            )
            stacked = stacked.reshape(-1, 3 * channels)
            total = total + jnp.dot(
                stacked,
                weight[step_t, step_r].reshape(3 * channels, outs),
                preferred_element_type=jnp.float32,
            )
    return total.reshape(frames, height, width, outs)


def per_device(latents, clip_index, first_conv, first_gain, middle_conv, head_gain, head_weight):
    place = lax.axis_index("tile")
    tile_count = lax.axis_size("tile")
    offset = STRIPS // 2 - 1
    rotated = (place - offset) % tile_count
    column = rotated % STRIPS
    block = rotated // STRIPS
    seq_column = place % STRIPS
    shard_rows = latents.shape[0]
    pieces = latents.reshape(shard_rows, CLAT, STRIPS, WS).transpose(2, 0, 1, 3)
    order = jnp.bitwise_xor(seq_column, jnp.arange(STRIPS, dtype=jnp.int32))
    buffer = jnp.take(pieces, order, axis=0)
    for bit in range(STRIPS.bit_length() - 1):
        view = buffer.reshape((STRIPS >> bit + 1, 2, 1 << bit) + buffer.shape[1:])
        came = partner(view[:, 1], "tile", bit)
        buffer = jnp.stack([view[:, 0], came], axis=1).reshape(buffer.shape)
    gathered = jnp.take(buffer, order, axis=0)
    gathered = shifted(gathered, "tile", offset)
    video = gathered.reshape(TF, HL, CLAT, WS).transpose(0, 1, 3, 2)
    padded_ids = jnp.concatenate([jnp.full((4,), -1, jnp.int32), clip_index])
    window = lax.dynamic_slice_in_dim(padded_ids, block * TF + 2, TF + 2)
    keep = jnp.stack([window[step_t : step_t + TF] == window[2:] for step_t in range(3)], axis=1)
    first = causal_conv(extend(video, column, None), keep, first_conv).astype(jnp.bfloat16)
    active = norm_act(first.astype(jnp.float32), first_gain).astype(jnp.bfloat16)
    summed = first.astype(jnp.float32) + causal_conv(
        extend(active, column, None), keep, middle_conv
    )
    outward = norm_act(summed, head_gain).astype(jnp.bfloat16)
    patch = jnp.dot(outward.reshape(-1, CH), head_weight, preferred_element_type=jnp.float32)
    patch = patch.reshape(TF, HL, WS, 3, PATCH)
    half = PATCH // 2
    front = patch[..., :half]
    back = patch[..., half:]
    arrived = shifted(back[:, :, -1], "tile", 1)
    arrived = jnp.where(column > 0, arrived, jnp.zeros_like(arrived))
    moved = jnp.concatenate([arrived[:, :, None], back[:, :, :-1]], axis=2)
    picture = (front + moved).transpose(0, 3, 1, 2, 4)
    return picture.reshape(1, TF, 3, HL, WS * half)


def solution(mesh):
    placed = (P(("group", "tile"), None, None), P("group"), P(), P(), P(), P(), P())
    return jax.shard_map(
        per_device,
        mesh=mesh,
        in_specs=placed,
        out_specs=P(("group", "tile"), None, None, None, None),
        check_vma=False,
    )
```

profile of v0, /device:TPU:0, one launch (start us, length us, event | category | flops | bytes accessed | tf_op | source)
XLA Modules:
  0.0 194.8 jit_solution(11909733101809147580)
XLA Ops:
  0.0 1.1 reshape.120
  1.2 0.6 gather_fusion
  2.0 0.6 collective-permute-start
  2.5 1.1 collective-permute-done
  3.7 2.9 %collective-permute-start.1 = (bf16[2,2,12,16,16]{4,3,2,0,1:T(8,128)(2,1)S(1)}, bf16[2,2,12,16,16]{4,3,2,0,1:T(8,128)(2,1)S(1)}, u32[]{:S(2)}, u32[]{:S(2)}) collective-permute-start(bf16[2,2,12,16,16]{4,3,2,0,1:T(8,128)(2,1)S(1)} %get-tuple-element.46), channel_id=1, source_target_pairs={{0,2},{1,3},{2,0},{3,1},{4,6},{5,7},{6,4},{7,5},{8,10},{9,11},{10,... | collective-permute-start | bytes 73736 | tf_op jit(solution)/shard_map/ppermute | solution.py:21
  6.6 5.2 %collective-permute-done.1 = bf16[2,2,12,16,16]{4,3,2,0,1:T(8,128)(2,1)S(1)} collective-permute-done((bf16[2,2,12,16,16]{4,3,2,0,1:T(8,128)(2,1)S(1)}, bf16[2,2,12,16,16]{4,3,2,0,1:T(8,128)(2,1)S(1)}, u32[]{:S(2)}, u32[]{:S(2)}) %collective-permute-start.1) | collective-permute-done | bytes 24608 | tf_op jit(solution)/shard_map/ppermute | solution.py:21
  12.0 1.9 collective-permute-start.2
  13.9 0.7 fusion.28
  14.6 3.9 %collective-permute-done.2 = bf16[1,4,12,16,16]{4,3,2,1,0:T(8,128)(2,1)S(1)} collective-permute-done((bf16[1,4,12,16,16]{4,3,2,1,0:T(8,128)(2,1)S(1)}, bf16[1,4,12,16,16]{4,3,2,1,0:T(8,128)(2,1)S(1)}, u32[]{:S(2)}, u32[]{:S(2)}) %collective-permute-start.2) | collective-permute-done | bytes 24608 | tf_op jit(solution)/shard_map/ppermute | solution.py:21
  18.5 0.6 gather_fusion.1
  19.4 8.9 %collective-permute-done.3 = bf16[8,12,16,16]{3,2,1,0:T(8,128)(2,1)S(1)} collective-permute-done((bf16[8,12,16,16]{3,2,1,0:T(8,128)(2,1)S(1)}, bf16[8,12,16,16]{3,2,1,0:T(8,128)(2,1)S(1)}, u32[]{:S(2)}, u32[]{:S(2)}) %collective-permute-start.3) | collective-permute-done | bytes 49184 | tf_op jit(solution)/shard_map/ppermute | solution.py:17
  28.7 4.1 %collective-permute-start.8 = (bf16[2,48,1,16]{1,0,2,3:T(2,128)(2,1)S(1)}, bf16[2,48,1,16]{1,0,2,3:T(2,128)(2,1)S(1)}, u32[]{:S(2)}, u32[]{:S(2)}) collective-permute-start(bf16[2,48,1,16]{1,0,2,3:T(2,128)(2,1)S(1)} %get-tuple-element.85), channel_id=1, source_target_pairs={{0,15},{1,0},{2,1},{3,2},{4,3},{5,4},{6,5},{7,6},{8,7},{9,8},{10,9... | collective-permute-start | bytes 9224 | tf_op jit(solution)/shard_map/ppermute | solution.py:17
  33.0 2.6 %collective-permute-start.5 = (bf16[2,48,16,16]{1,0,2,3:T(2,128)(2,1)S(1)}, bf16[2,48,16,16]{1,0,2,3:T(2,128)(2,1)S(1)}, u32[]{:S(2)}, u32[]{:S(2)}) collective-permute-start(bf16[2,48,16,16]{1,0,2,3:T(2,128)(2,1)S(1)} %bitcast.144), channel_id=1, source_target_pairs={{0,8},{1,9},{2,10},{3,11},{4,12},{5,13},{6,14},{7,15},{8,0},{9,1},... | collective-permute-start | bytes 147464 | tf_op jit(solution)/shard_map/ppermute | solution.py:17
  35.8 3.0 %collective-permute-start.4 = (bf16[2,48,1,16]{1,0,2,3:T(2,128)(2,1)S(1)}, bf16[2,48,1,16]{1,0,2,3:T(2,128)(2,1)S(1)}, u32[]{:S(2)}, u32[]{:S(2)}) collective-permute-start(bf16[2,48,1,16]{1,0,2,3:T(2,128)(2,1)S(1)} %get-tuple-element.84), channel_id=1, source_target_pairs={{0,9},{1,10},{2,11},{3,12},{4,13},{5,14},{6,15},{7,0},{8,1},{9,2},... | collective-permute-start | bytes 9224 | tf_op jit(solution)/shard_map/ppermute | solution.py:17
  38.8 2.7 %collective-permute-done.7 = bf16[2,48,1,16]{1,0,2,3:T(2,128)(2,1)S(1)} collective-permute-done((bf16[2,48,1,16]{1,0,2,3:T(2,128)(2,1)S(1)}, bf16[2,48,1,16]{1,0,2,3:T(2,128)(2,1)S(1)}, u32[]{:S(2)}, u32[]{:S(2)}) %collective-permute-start.7) | collective-permute-done | bytes 3104 | tf_op jit(solution)/shard_map/ppermute | solution.py:17
  41.5 0.7 fusion.13
  42.3 0.6 copy.136
  43.6 0.8 fusion.29
  44.6 1.3 fusion.30
  46.0 1.1 copy.129
  48.8 1.1 pad_maximum_fusion.19
  50.3 1.8 pad_maximum_fusion.20
  52.5 1.3 copy.137
  53.8 1.4 fusion.33
  60.7 0.7 multiply_convert_fusion.1
  61.7 2.6 %collective-permute-start.13 = (bf16[2,48,1,384]{3,2,1,0:T(2,128)(2,1)S(1)}, bf16[2,48,1,384]{3,2,1,0:T(2,128)(2,1)S(1)}, u32[]{:S(2)}, u32[]{:S(2)}) collective-permute-start(bf16[2,48,1,384]{3,2,1,0:T(2,128)(2,1)S(1)} %get-tuple-element.42), channel_id=1, source_target_pairs={{0,15},{1,0},{2,1},{3,2},{4,3},{5,4},{6,5},{7,6},{8,7},{9,8},{10,9... | collective-permute-start | bytes 221192 | tf_op jit(solution)/shard_map/ppermute | solution.py:17
  64.3 5.6 %fusion.21 = (bf16[1,1,3,384,384]{4,3,2,1,0:T(8,128)(2,1)S(1)}, bf16[1,1,3,384,384]{4,3,2,1,0:T(8,128)(2,1)}, bf16[1,1,3,384,384]{4,3,2,1,0:T(8,128)(2,1)}, bf16...) fusion(bf16[3,3,3,384,384]{4,3,2,1,0:T(8,128)(2,1)} %param.13), kind=kLoop, calls=%fused_computation.104 | loop fusion | bytes 15925248 | tf_op jit(solution)/shard_map/slice | solution.py:65
  70.0 0.6 collective-permute-start.10
  70.5 2.2 %collective-permute-start.12 = (bf16[2,48,1,384]{3,2,1,0:T(2,128)(2,1)S(1)}, bf16[2,48,1,384]{3,2,1,0:T(2,128)(2,1)S(1)}, u32[]{:S(2)}, u32[]{:S(2)}) collective-permute-start(bf16[2,48,1,384]{3,2,1,0:T(2,128)(2,1)S(1)} %get-tuple-element.41), channel_id=1, source_target_pairs={{0,1},{1,2},{2,3},{3,4},{4,5},{5,6},{6,7},{7,8},{8,9},{9,10},{10,1... | collective-permute-start | bytes 221192 | tf_op jit(solution)/shard_map/ppermute | solution.py:17
  73.4 34.5 %collective-permute-done.11 = bf16[2,48,1,384]{3,2,1,0:T(2,128)(2,1)S(1)} collective-permute-done((bf16[2,48,1,384]{3,2,1,0:T(2,128)(2,1)S(1)}, bf16[2,48,1,384]{3,2,1,0:T(2,128)(2,1)S(1)}, u32[]{:S(2)}, u32[]{:S(2)}) %collective-permute-start.11) | collective-permute-done | bytes 73760 | tf_op jit(solution)/shard_map/ppermute | solution.py:17
  108.5 1.8 fusion.5
  110.2 21.1 %collective-permute-done.10 = bf16[2,48,16,384]{3,2,1,0:T(8,128)(2,1)S(1)} collective-permute-done((bf16[2,48,16,384]{3,2,1,0:T(8,128)(2,1)S(1)}, bf16[2,48,16,384]{3,2,1,0:T(8,128)(2,1)S(1)}, u32[]{:S(2)}, u32[]{:S(2)}) %collective-permute-start.10) | collective-permute-done | bytes 1179680 | tf_op jit(solution)/shard_map/ppermute | solution.py:17
  131.4 2.3 %fusion.1 = bf16[4,50,18,384]{3,2,1,0:T(8,128)(2,1)S(1)} fusion(bf16[2,48,1,384]{3,2,1,0:T(2,128)(2,1)S(1)} %broadcast_select_fusion.2, bf16[2,48,1,384]{3,2,1,0:T(2,128)(2,1)S(1)} %broadcast_select_fusion.3, bf16[2,48,16,384]{3,2,1,0:T(8,128)(2,1)S(1)} %multiply_convert_fusion.1, bf16[2,48,1,384]{3,2,1,0:T(2,128)(2,1)S(1)} %broadcast_select_fusion.4, ...), kind=kLoop, calls=%fused_computation.6 | loop fusion | flops 29030400 | bytes 5419008 | tf_op jit(solution)/shard_map/concatenate | solution.py:41
  133.7 1.7 fusion.22
  135.8 4.3 %fusion.24 = (bf16[2,48,16,384]{3,2,1,0:T(8,128)(2,1)S(1)}, bf16[2,48,16,384]{3,2,1,0:T(8,128)(2,1)S(1)}, bf16[2,48,16,384]{3,2,1,0:T(8,128)(2,1)S(1)}, bf16[2,4...) fusion(bf16[2,50,18,384]{3,2,1,0:T(8,128)(2,1)S(1)} %get-tuple-, ...), kind=kLoop, calls=%fused_computation.107 | loop fusion | bytes 21233664 | tf_op jit(solution)/shard_map/slice | solution.py:60
  140.1 2.4 %fusion.23 = (bf16[2,48,16,384]{3,2,1,0:T(8,128)(2,1)S(1)}, bf16[2,48,16,384]{3,2,1,0:T(8,128)(2,1)S(1)}, bf16[2,48,16,384]{3,2,1,0:T(8,128)(2,1)S(1)}, bf16[2,4...) fusion(bf16[2,50,18,384]{3,2,1,0:T(8,128)(2,1)S(1)} %get-tuple-, ...), kind=kLoop, calls=%fused_computation.106 | loop fusion | bytes 21233664 | tf_op jit(solution)/shard_map/slice | solution.py:60
  142.9 0.8 copy-done.14
  143.7 2.1 %fusion.35 = f32[1536,384]{1,0:T(8,128)S(1)} fusion(bf16[1536,1152]{1,0:T(8,128)(2,1)S(1)} %bitcast.125, bf16[1152,384]{1,0:T(8,128)(2,1)S(1)} %bitcast.153), kind=kOutput, calls=%fused_computation.118 | convolution fusion | flops 1358954496 | bytes 6782976 | tf_op jit(solution)/shard_map/dot_general | solution.py:63
  146.2 0.8 copy-done.13
  147.0 2.1 %fusion.34 = f32[1536,384]{1,0:T(8,128)S(1)} fusion(bf16[1536,1152]{1,0:T(8,128)(2,1)S(1)} %bitcast.126, bf16[1152,384]{1,0:T(8,128)(2,1)S(1)} %bitcast.152), kind=kOutput, calls=%fused_computation.117 | convolution fusion | flops 1358954496 | bytes 6782976 | tf_op jit(solution)/shard_map/dot_general | solution.py:63
  149.5 0.8 copy-done.12
  150.3 2.1 %convolution_add_fusion.14 = f32[1536,384]{1,0:T(8,128)S(1)} fusion(f32[1536,384]{1,0:T(8,128)S(1)} %fusion.34, bf16[1536,1152]{1,0:T(8,128)(2,1)S(1)} %bitcast.119, bf16[1152,384]{1,0:T(8,128)(2,1)S(1)} %bitcast.151), kind=kOutput, calls=%fused_computation.40 | convolution fusion | flops 1359544320 | bytes 9142272 | tf_op jit(solution)/shard_map/dot_general | solution.py:63
  152.4 0.6 pad_maximum_fusion.4
  153.6 2.1 %convolution_add_fusion.13 = f32[1536,384]{1,0:T(8,128)S(1)} fusion(f32[1536,384]{1,0:T(8,128)S(1)} %convolution_add_fusion.14, bf16[1536,1152]{1,0:T(8,128)(2,1)S(1)} %bitcast.120, bf16[1152,384]{1,0:T(8,128)(2,1)S(1)} %bitcast.150), kind=kOutput, calls=%fused_computation.39 | convolution fusion | flops 1359544320 | bytes 9142272 | tf_op jit(solution)/shard_map/dot_general | solution.py:63
  156.1 0.8 copy-done.10
  156.9 2.2 %convolution_add_fusion.12 = f32[1536,384]{1,0:T(8,128)S(1)} fusion(f32[1536,384]{1,0:T(8,128)S(1)} %convolution_add_fusion.13, bf16[1536,1152]{1,0:T(8,128)(2,1)S(1)} %bitcast.121, bf16[1152,384]{1,0:T(8,128)(2,1)S(1)} %bitcast.149), kind=kOutput, calls=%fused_computation.38 | convolution fusion | flops 1359544320 | bytes 9142272 | tf_op jit(solution)/shard_map/dot_general | solution.py:63
  159.4 0.8 copy-done.9
  160.2 2.1 %convolution_add_fusion.11 = f32[1536,384]{1,0:T(8,128)S(1)} fusion(f32[1536,384]{1,0:T(8,128)S(1)} %convolution_add_fusion.12, bf16[1536,1152]{1,0:T(8,128)(2,1)S(1)} %bitcast.122, bf16[1152,384]{1,0:T(8,128)(2,1)S(1)} %bitcast.148), kind=kOutput, calls=%fused_computation.37 | convolution fusion | flops 1359544320 | bytes 9142272 | tf_op jit(solution)/shard_map/dot_general | solution.py:63
  162.7 0.8 copy-done.8
  163.5 2.1 %convolution_add_fusion.10 = f32[1536,384]{1,0:T(8,128)S(1)} fusion(f32[1536,384]{1,0:T(8,128)S(1)} %convolution_add_fusion.11, bf16[1536,1152]{1,0:T(8,128)(2,1)S(1)} %bitcast.123, bf16[1152,384]{1,0:T(8,128)(2,1)S(1)} %bitcast.147), kind=kOutput, calls=%fused_computation.36 | convolution fusion | flops 1359544320 | bytes 9142272 | tf_op jit(solution)/shard_map/dot_general | solution.py:63
  165.6 0.6 pad_maximum_fusion.8
  166.8 2.1 %convolution_add_fusion.9 = f32[1536,384]{1,0:T(8,128)S(1)} fusion(f32[1536,384]{1,0:T(8,128)S(1)} %convolution_add_fusion.10, bf16[1536,1152]{1,0:T(8,128)(2,1)S(1)} %bitcast.124, bf16[1152,384]{1,0:T(8,128)(2,1)S(1)} %bitcast.146), kind=kOutput, calls=%fused_computation.35 | convolution fusion | flops 1359544320 | bytes 9142272 | tf_op jit(solution)/shard_map/dot_general | solution.py:63
  168.9 2.6 %multiply_reduce_fusion = (f32[1536]{0:T(1024)S(1)}, f32[1536,384]{1,0:T(8,128)S(1)}) fusion(f32[1536,384]{1,0:T(8,128)S(1)} %get-tuple-element.89, f32[1536,384]{1,0:T(8,128)S(1)} %fusion.35, f32[1536,384]{1,0:T(8,128)S(1)} %convolution_add_fusion.9, bf16[1536,1152]{1,0:T(8,128)(2,1)S(1)} %bitcast.117, bf16[1152,384]{1,0:T(8,128)(2,1)S(1)} %bitcast.127), kind=kOutput, calls=%fused_computation.44 | convolution fusion | flops 1361902080 | bytes 13867008 | tf_op jit(solution)/shard_map/dot_general | solution.py:63
  171.6 0.7 multiply_convert_fusion
  172.3 2.2 %fusion.36 = f32[2,48,16,3,16]{2,4,3,1,0:T(8,128)S(1)} fusion(bf16[2,48,16,384,1]{3,2,4,1,0:T(8,128)(2,1)S(1)} %bitcast.118, bf16[3,16,384,1,1]{2,1,0,4,3:T(8,128)(2,1)S(1)} %bitcast.115), kind=kOutput, calls=%fused_computation.119 | convolution fusion | flops 56623104 | bytes 1511424 | tf_op jit(solution)/shard_map/dot_general | solution.py:99
  174.6 1.5 slice.547
  176.0 1.7 copy.138
  177.8 5.0 %collective-permute-start.14 = (f32[2,48,3,8]{1,3,2,0:T(8,128)S(1)}, f32[2,48,3,8]{1,3,2,0:T(8,128)S(1)}, u32[]{:S(2)}, u32[]{:S(2)}) collective-permute-start(f32[2,48,3,8]{1,3,2,0:T(8,128)S(1)} %bitcast.168), channel_id=1, source_target_pairs={{0,1},{1,2},{2,3},{3,4},{4,5},{5,6},{6,7},{7,8},{8,9},{9,10},{10,1... | collective-permute-start | bytes 27656 | tf_op jit(solution)/shard_map/ppermute | solution.py:17
  182.7 1.2 slice.548
  183.9 3.6 %collective-permute-done.14 = f32[2,48,3,8]{1,3,2,0:T(8,128)S(1)} collective-permute-done((f32[2,48,3,8]{1,3,2,0:T(8,128)S(1)}, f32[2,48,3,8]{1,3,2,0:T(8,128)S(1)}, u32[]{:S(2)}, u32[]{:S(2)}) %collective-permute-start.14) | collective-permute-done | bytes 9248 | tf_op jit(solution)/shard_map/ppermute | solution.py:17
  187.5 1.5 copy.139
  189.0 3.1 %fusion.11 = f32[2,3,48,16,8]{3,4,1,2,0:T(8,128)} fusion(f32[2,48,16,3,16]{2,4,3,1,0:T(8,128)S(1)} %fusion.36, f32[2,48,15,3,8]{2,4,3,1,0:T(8,128)} %slice.548, f32[2,48,1,3,8]{2,4,3,1,0:T(8,128)} %copy.139), kind=kLoop, calls=%fused_computation.50 | loop fusion | flops 73728 | bytes 442368 | tf_op jit(solution)/shard_map/transpose | solution.py:107
  192.1 1.6 copy.140
  193.7 0.8 copy.141
  (127 shorter events, 15.5 us)
Async XLA Ops:
  0.0 172.3 %copy-start = (bf16[384,48]{0,1:T(8,128)(2,1)S(1)}, bf16[384,48]{0,1:T(8,128)(2,1)}, u32[]{:S(2)}) copy-start(bf16[384,48]{0,1:T(8,128)(2,1)} %param.15) | copy-start | bytes 110596
  1.8 12.1 %copy-start.15 = (bf16[3,3,3,16,384]{4,3,2,1,0:T(8,128)(2,1)S(1)}, bf16[3,3,3,16,384]{4,3,2,1,0:T(8,128)(2,1)}, u32[]{:S(2)}) copy-start(bf16[3,3,3,16,384]{4,3,2,1,0:T(8,128)(2,1)} %param.11) | copy-start | bytes 995332
  2.0 1.6 collective-permute-start
  3.7 8.1 %collective-permute-start.1 = (bf16[2,2,12,16,16]{4,3,2,0,1:T(8,128)(2,1)S(1)}, bf16[2,2,12,16,16]{4,3,2,0,1:T(8,128)(2,1)S(1)}, u32[]{:S(2)}, u32[]{:S(2)}) collective-permute-start(bf16[2,2,12,16,16]{4,3,2,0,1:T(8,128)(2,1)S(1)} %get-tuple-element.46), channel_id=1, source_target_pairs={{0,2},{1,3},{2,0},{3,1},{4,6},{5,7},{6,4},{7,5},{8,10},{9,11},{10,... | collective-permute-start | bytes 73736 | tf_op jit(solution)/shard_map/ppermute | solution.py:21
  11.9 7.4 %copy-start.28 = (s32[4]{0:T(128)S(1)}, s32[4]{0:T(128)}, u32[]{:S(2)}) copy-start(s32[4]{0:T(128)} %param.10) | copy-start | bytes 52
  12.0 6.4 %collective-permute-start.2 = (bf16[1,4,12,16,16]{4,3,2,1,0:T(8,128)(2,1)S(1)}, bf16[1,4,12,16,16]{4,3,2,1,0:T(8,128)(2,1)S(1)}, u32[]{:S(2)}, u32[]{:S(2)}) collective-permute-start(bf16[1,4,12,16,16]{4,3,2,1,0:T(8,128)(2,1)S(1)} %get-tuple-element.44), channel_id=1, source_target_pairs={{0,4},{1,5},{2,6},{3,7},{4,0},{5,1},{6,2},{7,3},{8,12},{9,13},{10,... | collective-permute-start | bytes 73736 | tf_op jit(solution)/shard_map/ppermute | solution.py:21
  19.3 9.1 %collective-permute-start.3 = (bf16[8,12,16,16]{3,2,1,0:T(8,128)(2,1)S(1)}, bf16[8,12,16,16]{3,2,1,0:T(8,128)(2,1)S(1)}, u32[]{:S(2)}, u32[]{:S(2)}) collective-permute-start(bf16[8,12,16,16]{3,2,1,0:T(8,128)(2,1)S(1)} %broadcast_select_fusion.1), channel_id=1, source_target_pairs={{0,3},{1,4},{2,5},{3,6},{4,7},{5,8},{6,9},{7,10},{8,11},{9,12},{10... | collective-permute-start | bytes 147464 | tf_op jit(solution)/shard_map/ppermute | solution.py:17
  28.7 10.0 %collective-permute-start.8 = (bf16[2,48,1,16]{1,0,2,3:T(2,128)(2,1)S(1)}, bf16[2,48,1,16]{1,0,2,3:T(2,128)(2,1)S(1)}, u32[]{:S(2)}, u32[]{:S(2)}) collective-permute-start(bf16[2,48,1,16]{1,0,2,3:T(2,128)(2,1)S(1)} %get-tuple-element.85), channel_id=1, source_target_pairs={{0,15},{1,0},{2,1},{3,2},{4,3},{5,4},{6,5},{7,6},{8,7},{9,8},{10,9... | collective-permute-start | bytes 9224 | tf_op jit(solution)/shard_map/ppermute | solution.py:17
  32.9 11.7 %copy-start.22 = (bf16[2]{0:T(256)(128)(2,1)}, bf16[2]{0:T(256)(128)(2,1)S(1)}, u32[]{:S(2)}) copy-start(bf16[2]{0:T(256)(128)(2,1)S(1)} %get-tuple-element.86) | copy-start | bytes 16
  32.9 11.7 %copy-start.24 = (bf16[2]{0:T(256)(128)(2,1)}, bf16[2]{0:T(256)(128)(2,1)S(1)}, u32[]{:S(2)}) copy-start(bf16[2]{0:T(256)(128)(2,1)S(1)} %get-tuple-element.87) | copy-start | bytes 16
  32.9 5.9 %collective-permute-start.6 = (bf16[2,48,1,16]{1,0,2,3:T(2,128)(2,1)S(1)}, bf16[2,48,1,16]{1,0,2,3:T(2,128)(2,1)S(1)}, u32[]{:S(2)}, u32[]{:S(2)}) collective-permute-start(bf16[2,48,1,16]{1,0,2,3:T(2,128)(2,1)S(1)} %get-tuple-element.85), channel_id=1, source_target_pairs={{0,7},{1,8},{2,9},{3,10},{4,11},{5,12},{6,13},{7,14},{8,15},{9,0},... | collective-permute-start | bytes 9224 | tf_op jit(solution)/shard_map/ppermute | solution.py:17
  33.0 10.4 %collective-permute-start.5 = (bf16[2,48,16,16]{1,0,2,3:T(2,128)(2,1)S(1)}, bf16[2,48,16,16]{1,0,2,3:T(2,128)(2,1)S(1)}, u32[]{:S(2)}, u32[]{:S(2)}) collective-permute-start(bf16[2,48,16,16]{1,0,2,3:T(2,128)(2,1)S(1)} %bitcast.144), channel_id=1, source_target_pairs={{0,8},{1,9},{2,10},{3,11},{4,12},{5,13},{6,14},{7,15},{8,0},{9,1},... | collective-permute-start | bytes 147464 | tf_op jit(solution)/shard_map/ppermute | solution.py:17
  35.6 5.9 %collective-permute-start.7 = (bf16[2,48,1,16]{1,0,2,3:T(2,128)(2,1)S(1)}, bf16[2,48,1,16]{1,0,2,3:T(2,128)(2,1)S(1)}, u32[]{:S(2)}, u32[]{:S(2)}) collective-permute-start(bf16[2,48,1,16]{1,0,2,3:T(2,128)(2,1)S(1)} %get-tuple-element.84), channel_id=1, source_target_pairs={{0,1},{1,2},{2,3},{3,4},{4,5},{5,6},{6,7},{7,8},{8,9},{9,10},{10,1... | collective-permute-start | bytes 9224 | tf_op jit(solution)/shard_map/ppermute | solution.py:17
  35.8 5.8 %collective-permute-start.4 = (bf16[2,48,1,16]{1,0,2,3:T(2,128)(2,1)S(1)}, bf16[2,48,1,16]{1,0,2,3:T(2,128)(2,1)S(1)}, u32[]{:S(2)}, u32[]{:S(2)}) collective-permute-start(bf16[2,48,1,16]{1,0,2,3:T(2,128)(2,1)S(1)} %get-tuple-element.84), channel_id=1, source_target_pairs={{0,9},{1,10},{2,11},{3,12},{4,13},{5,14},{6,15},{7,0},{8,1},{9,2},... | collective-permute-start | bytes 9224 | tf_op jit(solution)/shard_map/ppermute | solution.py:17
  52.1 3.1 %copy-start.21 = (bf16[1,1,3,16,384]{4,3,2,1,0:T(8,128)(2,1)S(1)}, bf16[1,1,3,16,384]{4,3,2,1,0:T(8,128)(2,1)}, u32[]{:S(2)}) copy-start(bf16[1,1,3,16,384]{4,3,2,1,0:T(8,128)(2,1)} %get-tuple-element.55) | copy-start | bytes 110596
  55.3 0.8 copy-start.20
  56.0 0.8 copy-start.19
  56.8 0.8 copy-start.18
  57.6 0.8 copy-start.17
  58.4 0.8 copy-start.16
  60.0 0.7 copy-start.26
  61.7 11.6 %collective-permute-start.13 = (bf16[2,48,1,384]{3,2,1,0:T(2,128)(2,1)S(1)}, bf16[2,48,1,384]{3,2,1,0:T(2,128)(2,1)S(1)}, u32[]{:S(2)}, u32[]{:S(2)}) collective-permute-start(bf16[2,48,1,384]{3,2,1,0:T(2,128)(2,1)S(1)} %get-tuple-element.42), channel_id=1, source_target_pairs={{0,15},{1,0},{2,1},{3,2},{4,3},{5,4},{6,5},{7,6},{8,7},{9,8},{10,9... | collective-permute-start | bytes 221192 | tf_op jit(solution)/shard_map/ppermute | solution.py:17
  69.9 38.0 %collective-permute-start.11 = (bf16[2,48,1,384]{3,2,1,0:T(2,128)(2,1)S(1)}, bf16[2,48,1,384]{3,2,1,0:T(2,128)(2,1)S(1)}, u32[]{:S(2)}, u32[]{:S(2)}) collective-permute-start(bf16[2,48,1,384]{3,2,1,0:T(2,128)(2,1)S(1)} %get-tuple-element.42), channel_id=1, source_target_pairs={{0,7},{1,8},{2,9},{3,10},{4,11},{5,12},{6,13},{7,14},{8,15},{9,0},... | collective-permute-start | bytes 221192 | tf_op jit(solution)/shard_map/ppermute | solution.py:17
  70.0 61.4 %collective-permute-start.10 = (bf16[2,48,16,384]{3,2,1,0:T(8,128)(2,1)S(1)}, bf16[2,48,16,384]{3,2,1,0:T(8,128)(2,1)S(1)}, u32[]{:S(2)}, u32[]{:S(2)}) collective-permute-start(bf16[2,48,16,384]{3,2,1,0:T(8,128)(2,1)S(1)} %multiply_convert_fusion.1), channel_id=1, source_target_pairs={{0,8},{1,9},{2,10},{3,11},{4,12},{5,13},{6,14},{7,15},{8,0},{9,1},... | collective-permute-start | bytes 3538952 | tf_op jit(solution)/shard_map/ppermute | solution.py:17
  70.5 37.6 %collective-permute-start.12 = (bf16[2,48,1,384]{3,2,1,0:T(2,128)(2,1)S(1)}, bf16[2,48,1,384]{3,2,1,0:T(2,128)(2,1)S(1)}, u32[]{:S(2)}, u32[]{:S(2)}) collective-permute-start(bf16[2,48,1,384]{3,2,1,0:T(2,128)(2,1)S(1)} %get-tuple-element.41), channel_id=1, source_target_pairs={{0,1},{1,2},{2,3},{3,4},{4,5},{5,6},{6,7},{7,8},{8,9},{9,10},{10,1... | collective-permute-start | bytes 221192 | tf_op jit(solution)/shard_map/ppermute | solution.py:17
  72.7 35.6 %collective-permute-start.9 = (bf16[2,48,1,384]{3,2,1,0:T(2,128)(2,1)S(1)}, bf16[2,48,1,384]{3,2,1,0:T(2,128)(2,1)S(1)}, u32[]{:S(2)}, u32[]{:S(2)}) collective-permute-start(bf16[2,48,1,384]{3,2,1,0:T(2,128)(2,1)S(1)} %get-tuple-element.41), channel_id=1, source_target_pairs={{0,9},{1,10},{2,11},{3,12},{4,13},{5,14},{6,15},{7,0},{8,1},{9,2},... | collective-permute-start | bytes 221192 | tf_op jit(solution)/shard_map/ppermute | solution.py:17
  133.7 1.7 copy-start.23
  133.7 1.7 copy-start.25
  142.5 1.2 copy-start.14
  143.7 2.1 %copy-start.4 = (bf16[2,48,16,384]{3,2,1,0:T(8,128)(2,1)S(1)}, bf16[2,48,16,384]{3,2,1,0:T(8,128)(2,1)}, u32[]{:S(2)}) copy-start(bf16[2,48,16,384]{3,2,1,0:T(8,128)(2,1)} %get-tuple-element.38) | copy-start | bytes 3538948
  143.7 2.1 %copy-start.5 = (bf16[2,48,16,384]{3,2,1,0:T(8,128)(2,1)S(1)}, bf16[2,48,16,384]{3,2,1,0:T(8,128)(2,1)}, u32[]{:S(2)}) copy-start(bf16[2,48,16,384]{3,2,1,0:T(8,128)(2,1)} %get-tuple-element.39) | copy-start | bytes 3538948
  143.7 2.1 %copy-start.6 = (bf16[2,48,16,384]{3,2,1,0:T(8,128)(2,1)S(1)}, bf16[2,48,16,384]{3,2,1,0:T(8,128)(2,1)}, u32[]{:S(2)}) copy-start(bf16[2,48,16,384]{3,2,1,0:T(8,128)(2,1)} %get-tuple-element.40) | copy-start | bytes 3538948
  145.8 1.2 copy-start.13
  147.0 2.1 %copy-start.1 = (bf16[2,48,16,384]{3,2,1,0:T(8,128)(2,1)S(1)}, bf16[2,48,16,384]{3,2,1,0:T(8,128)(2,1)}, u32[]{:S(2)}) copy-start(bf16[2,48,16,384]{3,2,1,0:T(8,128)(2,1)} %get-tuple-element.35) | copy-start | bytes 3538948
  147.0 2.1 %copy-start.2 = (bf16[2,48,16,384]{3,2,1,0:T(8,128)(2,1)S(1)}, bf16[2,48,16,384]{3,2,1,0:T(8,128)(2,1)}, u32[]{:S(2)}) copy-start(bf16[2,48,16,384]{3,2,1,0:T(8,128)(2,1)} %get-tuple-element.36) | copy-start | bytes 3538948
  147.0 2.1 %copy-start.3 = (bf16[2,48,16,384]{3,2,1,0:T(8,128)(2,1)S(1)}, bf16[2,48,16,384]{3,2,1,0:T(8,128)(2,1)}, u32[]{:S(2)}) copy-start(bf16[2,48,16,384]{3,2,1,0:T(8,128)(2,1)} %get-tuple-element.37) | copy-start | bytes 3538948
  149.2 1.2 copy-start.12
  152.4 1.2 copy-start.11
  155.7 1.2 copy-start.10
  159.1 1.2 copy-start.9
  162.3 1.2 copy-start.8
  165.6 1.2 copy-start.7
  168.9 2.7 %copy-start.27 = (f32[384]{0:T(512)S(1)}, f32[384]{0:T(512)}, u32[]{:S(2)}) copy-start(f32[384]{0:T(512)} %param.14) | copy-start | bytes 4612
  177.8 9.7 %collective-permute-start.14 = (f32[2,48,3,8]{1,3,2,0:T(8,128)S(1)}, f32[2,48,3,8]{1,3,2,0:T(8,128)S(1)}, u32[]{:S(2)}, u32[]{:S(2)}) collective-permute-start(f32[2,48,3,8]{1,3,2,0:T(8,128)S(1)} %bitcast.168), channel_id=1, source_target_pairs={{0,1},{1,2},{2,3},{3,4},{4,5},{5,6},{6,7},{7,8},{8,9},{9,10},{10,1... | collective-permute-start | bytes 27656 | tf_op jit(solution)/shard_map/ppermute | solution.py:17
where the time goes:
time: 198 us; the launch traced here: 195 us
  waiting for transfers between devices  81.5 us (41%)
  local copies, waits for them, and re-layouts  41.1 us (21%)
  matrix products  26.8 us (14%)
  starting transfers between devices  26.2 us (13%)
  other arithmetic  18.1 us (9%)
    ppermute x12, waiting for transfers between devices, shifted(): lax.ppermute(value, axis, [(i, (i + by) % length) for i in range(length)])  71.4 us
    dot_general x18, matrix products, causal_conv(): jnp.dot(stacked, weight[step_t, step_r].reshape(3 * channels, outs), pref...  24.6 us
    ppermute x12, starting transfers between devices, shifted(): lax.ppermute(value, axis, [(i, (i + by) % length) for i in range(length)])  20.8 us
    slice x5, local copies, waits for them, and re-layouts, causal_conv(): rows[:, :, step_c:step_c + width]  10.6 us
    ppermute x3, waiting for transfers between devices, partner(): lax.ppermute(value, axis, [(i, i ^ 1 << apart) for i in range(lax.axis_si...  10.1 us
    concatenate x17, other arithmetic, causal_conv(): jnp.concatenate([rows[:, :, step_c:step_c + width] for step_c in range(3)...  9.24 us
    unnamed x58, local copies, waits for them, and re-layouts  7.46 us
    slice x2, local copies, waits for them, and re-layouts, causal_conv(): weight[step_t, step_r].reshape(3 * channels, outs)  6.3 us
  transfers between devices with their start and end apart: 15, of which 9 were waited for; matrix products, arithmetic and copies ran while one was open for 6% of the time, Pallas kernels for 0%

commit v1 on v0

v1 whole, which is shorter than its diff:
```python
import jax
import jax.numpy as jnp
from jax import lax
from jax.experimental import pallas as pl
from jax.experimental.pallas import tpu as pltpu
from jax.sharding import PartitionSpec as P

WS = 16
TF = 2


def norm_act(x, gain):
    scale = lax.rsqrt(jnp.mean(x * x, axis=-1, keepdims=True) + 1e-06)
    v = x * scale * gain
    return v / (1.0 + jnp.exp(-v))


def row_shift(x, by):
    rows = lax.broadcasted_iota(jnp.int32, x.shape, 0)
    n = x.shape[0]
    if by > 0:
        return jnp.where(rows == 0, 0.0, pltpu.roll(x, 1, 0))
    return jnp.where(rows == n - 1, 0.0, pltpu.roll(x, n - 1, 0))


def decode_kernel(
    scal, z_ref, w1_ref, g1_ref, wm_hbm, g2_ref, hw_ref, out_ref,
    wm, act, firstb, fscr, acc, outw, sem,
):
    hl = z_ref.shape[2]
    ch = g1_ref.shape[-1]
    strips = scal[7]
    strip = scal[6]
    patch = hw_ref.shape[-1] // 3
    half = patch // 2
    aw = WS + 3
    ow = WS + 1
    lanes = WS * half

    def tap_copies(dt):
        return [
            pltpu.make_async_copy(
                wm_hbm.at[dt, dr, dc],
                wm.at[dt, pl.ds(dc * ch, ch), pl.ds(dr * ch, ch)],
                sem.at[dt],
            )
            for dr in range(3)
            for dc in range(3)
        ]

    for dt in (2, 1, 0):
        for copy in tap_copies(dt):
            copy.start()

    for f in range(TF + 2):
        if f == 0:
            needed = scal[2] == scal[4]
        elif f == 1:
            needed = jnp.logical_or(scal[3] == scal[4], scal[3] == scal[5])
        else:
            needed = scal[4] == scal[4]

        @pl.when(needed)
        def _(f=f):
            total = None
            for dt in range(3):
                keep = (scal[f + dt] == scal[f + 2]).astype(jnp.float32)
                lhs = z_ref[f + dt].reshape(aw * hl, z_ref.shape[-1])
                if dt < 2:
                    lhs = lhs * keep.astype(jnp.bfloat16)
                part = jnp.dot(lhs, w1_ref[dt], preferred_element_type=jnp.float32)
                total = part if total is None else total + part
            fscr[...] = total.reshape(aw, hl, ch)

            @pl.loop(0, aw)
            def _(w):
                rounded = fscr[w].astype(jnp.bfloat16)
                if f >= 2:
                    firstb[f - 2, w] = rounded
                value = norm_act(rounded.astype(jnp.float32), g1_ref[...])
                col = strip * WS + w - 2
                inside = jnp.logical_and(col >= 0, col < strips * WS).astype(jnp.float32)
                act[f, w] = (value * inside).astype(jnp.bfloat16)

    for dt in (2, 1, 0):
        for copy in tap_copies(dt):
            copy.wait()

        @pl.loop(0, TF)
        def _(fo, dt=dt):
            def unit():
                lhs = jnp.concatenate(
                    [act[fo + dt, pl.ds(dc, ow)].reshape(ow * hl, ch) for dc in range(3)], axis=-1
                )
                return jnp.dot(lhs, wm[dt], preferred_element_type=jnp.float32)

            if dt == 2:
                acc[fo] = unit()
            else:

                @pl.when(scal[fo + dt + 2] == scal[fo + 4])
                def _():
                    acc[fo] += unit()

    rows = lax.broadcasted_iota(jnp.int32, (3 * patch, 6 * lanes), 0)
    cols = lax.broadcasted_iota(jnp.int32, (3 * patch, 6 * lanes), 1)
    odd = cols // (3 * lanes)
    colour = (cols // lanes) % 3
    want = colour * patch + (cols % lanes + half * odd) % patch
    spread = (rows == want).astype(jnp.bfloat16)
    head = jnp.dot(hw_ref[...], spread, preferred_element_type=jnp.float32).astype(jnp.bfloat16)
    lane = lax.broadcasted_iota(jnp.int32, (hl, lanes), 1)

    for fo in range(TF):

        @pl.loop(0, ow)
        def _(w, fo=fo):
            start = pl.multiple_of(w * hl, hl)
            part = acc[fo, pl.ds(start, hl)]
            summed = (
                firstb[fo, w + 1].astype(jnp.float32)
                + row_shift(part[:, :ch], 1)
                + part[:, ch : 2 * ch]
                + row_shift(part[:, 2 * ch :], -1)
            )
            value = norm_act(summed, g2_ref[...])
            inside = jnp.logical_or(strip > 0, w > 0).astype(jnp.float32)
            outw[fo, w % 2, w // 2] = (value * inside).astype(jnp.bfloat16)

        p_odd = jnp.dot(
            outw[fo, 0].reshape(-1, ch), head[:, 3 * lanes :], preferred_element_type=jnp.float32
        )
        p_even = jnp.dot(
            outw[fo, 1, : WS // 2].reshape(-1, ch), head[:, : 3 * lanes],
            preferred_element_type=jnp.float32,
        )
        for k in range(3):
            front = jnp.zeros((hl, lanes), jnp.float32)
            back = jnp.zeros((hl, lanes), jnp.float32)
            for i in range(WS // 2):
                piece = p_even[i * hl : (i + 1) * hl, k * lanes : (k + 1) * lanes]
                front = jnp.where(lane // patch == i, piece, front)
            for i in range(WS // 2 + 1):
                piece = p_odd[i * hl : (i + 1) * hl, k * lanes : (k + 1) * lanes]
                back = jnp.where((lane + half) // patch == i, piece, back)
            out_ref[fo, k] = front + back


def per_device(latents, clip_index, first_conv, first_gain, middle_conv, head_gain, head_weight):
    place = lax.axis_index("tile")
    tiles = lax.axis_size("tile")
    shard_rows, clat, wl = latents.shape
    ch = first_gain.shape[0]
    frames = clip_index.shape[0]
    hl = tiles * shard_rows // frames
    strips = wl // WS
    half = head_weight.shape[1] // 6
    offset = strips // 2 - 1
    rotated = (place - offset) % tiles
    strip = rotated % strips
    block = rotated // strips

    full = lax.all_gather(latents, "tile", axis=0, tiled=True)
    full = full.reshape(frames, hl, clat, wl)
    full = jnp.pad(full, ((4, 0), (0, 0), (0, 0), (3, WS + 5)))
    aw = WS + 3
    win = lax.dynamic_slice(
        full, (block * TF, 0, 0, strip * WS), (TF + 4, hl, clat, WS + 5)
    ).transpose(0, 3, 1, 2)
    win = jnp.pad(win, ((0, 0), (0, 0), (1, 1), (0, 0)))
    z = jnp.concatenate(
        [win[:, dc : dc + aw, dr : dr + hl] for dr in range(3) for dc in range(3)], axis=-1
    )
    ids = jnp.concatenate([jnp.full((4,), -1, jnp.int32), clip_index])
    ids = lax.dynamic_slice_in_dim(ids, block * TF, TF + 4)
    scal = jnp.concatenate([ids, jnp.stack([strip, jnp.int32(strips)]).astype(jnp.int32)])
    vm = pl.BlockSpec(memory_space=pltpu.VMEM)
    out = pl.pallas_call(
        decode_kernel,
        out_shape=jax.ShapeDtypeStruct((TF, 3, hl, WS * half), jnp.float32),
        in_specs=[
            pl.BlockSpec(memory_space=pltpu.SMEM), vm, vm, vm,
            pl.BlockSpec(memory_space=pl.ANY), vm, vm,
        ],
        out_specs=vm,
        scratch_shapes=[
            pltpu.VMEM((3, 3 * ch, 3 * ch), jnp.bfloat16),
            pltpu.VMEM((TF + 2, aw, hl, ch), jnp.bfloat16),
            pltpu.VMEM((TF, aw, hl, ch), jnp.bfloat16),
            pltpu.VMEM((aw, hl, ch), jnp.float32),
            pltpu.VMEM((TF, (WS + 1) * hl, 3 * ch), jnp.float32),
            pltpu.VMEM((TF, 2, WS // 2 + 1, hl, ch), jnp.bfloat16),
            pltpu.SemaphoreType.DMA((3,)),
        ],
        compiler_params=pltpu.CompilerParams(vmem_limit_bytes=60 * 1024 * 1024),
    )(
        scal, z, first_conv.reshape(3, 9 * clat, ch), first_gain.reshape(1, ch), middle_conv,
        head_gain.reshape(1, ch), head_weight,
    )
    return out[None]


def solution(mesh):
    placed = (P(("group", "tile"), None, None), P("group"), P(), P(), P(), P(), P())
    return jax.shard_map(
        per_device,
        mesh=mesh,
        in_specs=placed,
        out_specs=P(("group", "tile"), None, None, None, None),
        check_vma=False,
    )
```

time: 198 us -> 88.2 us (0.45)
  the two profiles are of different devices: /device:TPU:0 before, /device:TPU:3 now
where the time goes in v1:
time: 88.2 us; the launch traced here: 87.1 us
  Pallas kernels  33.5 us (38%)
  local copies, waits for them, and re-layouts  28.1 us (32%)
  blocking collectives  24.7 us (28%)
    pallas_call x1, Pallas kernels, per_device(): pl.pallas_call(decode_kernel, out_shape=jax.ShapeDtypeStruct((TF, 3, hl,...  33.5 us
    all_gather x1, blocking collectives, per_device(): full = lax.all_gather(latents, 'tile', axis=0, tiled=True)  24.7 us
    concatenate x1, local copies, waits for them, and re-layouts, per_device(): jnp.concatenate([win[:, dc:dc + aw, dr:dr + hl] for dr in range(3) for dc...  12.6 us
    reshape x1, local copies, waits for them, and re-layouts, per_device(): full = full.reshape(frames, hl, clat, wl)  6.03 us
    slice x1, local copies, waits for them, and re-layouts, per_device(): win[:, dc:dc + aw, dr:dr + hl]  4.84 us
    transpose x1, local copies, waits for them, and re-layouts, per_device(): win = lax.dynamic_slice(full, (block * TF, 0, 0, strip * WS), (TF + 4, hl...  2.03 us

profile of v1, /device:TPU:3, one launch (start us, length us, event | category | flops | bytes accessed | tf_op | source)
XLA Modules:
  0.0 87.1 jit_solution(9098893868606640295)
XLA Ops:
  0.0 0.7 pad_dynamic-slice_fusion.1
  0.7 0.6 pad_add_fusion.scal
  1.3 24.7 %all_gather.3 = bf16[192,16,128]{2,1,0:T(8,128)(2,1)S(1)} all-gather(bf16[12,16,128]{2,1,0:T(8,128)(2,1)} %param.7), channel_id=1, replica_groups=mesh['group'=2,'tile'=16] {'tile'}, dimensions={0}, use_global_device_ids=true | all-gather | bytes 835584 | tf_op jit(solution)/shard_map/all_gather | solution.py:163
  26.0 6.0 %copy.11 = bf16[4,48,16,128]{2,1,3,0:T(8,128)(2,1)} copy(bf16[4,48,16,128]{3,2,1,0:T(8,128)(2,1)S(1)} %bitcast.6) | data formatting | bytes 1572864 | tf_op jit(solution)/shard_map/reshape | solution.py:164
  32.1 2.0 %fusion = bf16[6,21,48,16]{3,2,1,0:T(8,128)(2,1)S(1)} fusion(s32[]{:T(128)S(6)} %select_n.24, s32[]{:T(128)S(6)} %select_n.26, bf16[4,48,16,128]{2,1,3,0:T(8,128)(2,1)} %copy.11), kind=kLoop, calls=%fused_computation.1 | loop fusion | bytes 979976 | tf_op jit(solution)/shard_map/transpose | solution.py:169
  34.1 4.8 %pad_slice_fusion = (bf16[6,19,48,16]{3,2,1,0:T(8,128)(2,1)S(1)}, bf16[6,19,48,16]{3,2,1,0:T(8,128)(2,1)S(1)}, bf16[6,19,48,16]{3,2,1,0:T(8,128)(2,1)}, bf16[6,1...) fusion(bf16[6,21,48,16]{3,2,1,0:T(8,128)(2,1)S(1)} %fusion), kind=kLoop, calls=%fused_computation.2 | loop fusion | bytes 7326720 | tf_op jit(solution)/shard_map/slice | solution.py:172
  38.9 0.0 copy-start.1
  39.0 0.0 copy-start.2
  39.0 0.0 copy-start
  39.0 12.6 %concatenate.11.z_ref = bf16[6,19,48,144]{3,2,1,0:T(8,128)(2,1)} concatenate(bf16[6,19,48,16]{3,2,1,0:T(8,128)(2,1)} %get-tuple-element.13, bf16[6,19,48,16]{3,2,1,0:T(8,128)(2,1)S(1)} %get-tuple-element.6, bf16[6,19,48,16]{3,2,1,0:T(8,128)(2,1)} %get-tuple-element.7, bf16[6,19,48,16]{3,2,1,0:T(8,128)(2,1)} %get-tuple-element.12, bf16[6,19,48,16]{3,2,1,0:T(8,128)(2,1)} %get-tuple-element.11, ...), dimensions={3} | concatenate | bytes 3151872 | tf_op jit(solution)/shard_map/concatenate | solution.py:171
  51.6 0.0 copy-done.1
  51.6 0.5 reshape.14.g1_ref
  52.1 0.0 copy-done.2
  52.1 0.5 reshape.15.g2_ref
  52.7 0.0 copy-done
  52.7 0.7 copy.12.hw_ref
  53.4 33.5 %shard_map.73 = f32[2,3,48,128]{3,2,1,0:T(8,128)} custom-call(s32[8]{0:T(128)} %pad_add_fusion.scal, bf16[6,19,48,144]{3,2,1,0:T(8,128)(2,1)} %concatenate.11.z_ref, bf16[3,144,384]{2,1,0:T(8,128)(2,1)} %bitcast.7, f32[1,384]{1,0:T(1,128)} %reshape.14.g1_ref, bf16[3,3,3,384,384]{4,3,2,1,0:T(8,128)(2,1)} %wm_hbm.1, f32[1,384]{1,0:T(1,128)} %reshape.15.g2_ref, ...), custom_call_target="tpu_custom_call" | custom-call | tf_op jit(solution)/shard_map/pallas_call | solution.py:178
Async XLA Ops:
  38.9 12.7 %copy-start.1 = (f32[384]{0:T(512)S(1)}, f32[384]{0:T(512)}, u32[]{:S(2)}) copy-start(f32[384]{0:T(512)} %param.10) | copy-start | bytes 4612
  39.0 13.2 %copy-start.2 = (f32[384]{0:T(512)S(1)}, f32[384]{0:T(512)}, u32[]{:S(2)}) copy-start(f32[384]{0:T(512)} %param.12) | copy-start | bytes 4612
  39.0 13.7 %copy-start = (bf16[384,48]{0,1:T(8,128)(2,1)S(1)}, bf16[384,48]{0,1:T(8,128)(2,1)}, u32[]{:S(2)}) copy-start(bf16[384,48]{0,1:T(8,128)(2,1)} %param.13) | copy-start | bytes 110596

commit v2 on v1

--- a/solution.py
+++ b/solution.py
@@ -1,3 +1,5 @@
+import functools
+
 import jax
 import jax.numpy as jnp
 from jax import lax
@@ -7,6 +9,8 @@
 
 WS = 16
 TF = 2
+LANES = 128
+GAP = LANES // 2
 
 
 def norm_act(x, gain):
@@ -23,19 +27,112 @@
     return jnp.where(rows == n - 1, 0.0, pltpu.roll(x, n - 1, 0))
 
 
+def exchange_kernel(sizes, lat_ref, got, pad_a, pad_b, stage, send_sem, recv_sem, own_sem):
+    tiles, strips, frames, shard_rows = sizes
+    quarters = tiles // frames
+    blocks = tiles // strips
+    offset = strips // 2 - 1
+    me = lax.axis_index("tile")
+    barrier = pltpu.get_barrier_semaphore()
+    for step in range(1, tiles):
+        pl.semaphore_signal(barrier, inc=1, device_id={"tile": lax.rem(me + step, tiles)})
+
+    wl = lat_ref.shape[1]
+    values = lat_ref[...].astype(jnp.float32)
+    spare = jnp.zeros((2 * LANES - values.shape[0], wl), jnp.float32)
+    for pad, rows in ((pad_a, values[:LANES]), (pad_b, jnp.concatenate([values[LANES:], spare]))):
+        pad[:8] = jnp.zeros((8, LANES), jnp.float32)
+        pad[8 + wl :] = jnp.zeros((WS, LANES), jnp.float32)
+        pad[8 : 8 + wl] = rows.T
+    low = lax.broadcasted_iota(jnp.int32, (WS, LANES), 1) < LANES // 2
+    for s in range(strips):
+        stage[s, : 2 * WS] = pad_a[WS * s : WS * (s + 2)].astype(jnp.bfloat16)
+        upper = pltpu.roll(pad_b[WS * (s + 1) : WS * (s + 2)], LANES // 2, 1)
+        mixed = jnp.where(low, pad_b[WS * s : WS * (s + 1)], upper)
+        stage[s, 2 * WS :] = mixed.astype(jnp.bfloat16)
+    pl.semaphore_wait(barrier, tiles - 1)
+
+    frame = me // quarters
+    quarter = me % quarters
+
+    def each_send(act):
+        for ahead in range(3):
+            block = frame // TF + ahead
+            slot = (2 * TF - TF * ahead + frame % TF) * quarters + quarter
+
+            @pl.when(block < blocks)
+            def _():
+                @pl.loop(0, strips)
+                def _(j):
+                    s = (j + me) % strips
+                    to = (block * strips + s + offset) % tiles
+
+                    @pl.when(to != me)
+                    def _():
+                        act(
+                            pltpu.make_async_remote_copy(
+                                src_ref=stage.at[s],
+                                dst_ref=got.at[slot],
+                                send_sem=send_sem.at[ahead * strips + s],
+                                recv_sem=recv_sem.at[slot],
+                                device_id={"tile": to},
+                            ),
+                            None,
+                        )
+
+                    @pl.when(to == me)
+                    def _():
+                        act(None, pltpu.make_async_copy(stage.at[s], got.at[slot], own_sem))
+
+    def start(remote, local):
+        (remote if local is None else local).start()
+
+    def finish(remote, local):
+        if local is None:
+            remote.wait_send()
+        else:
+            local.wait()
+
+    each_send(start)
+    mine = (me + tiles - offset) % tiles // strips
+
+    @pl.loop(0, 3 * TF * quarters)
+    def _(slot):
+        source = (TF * mine - 2 * TF) * quarters + slot
+
+        @pl.when(jnp.logical_and(source >= 0, source != me))
+        def _():
+            pltpu.make_async_remote_copy(
+                src_ref=stage.at[0],
+                dst_ref=got.at[slot],
+                send_sem=send_sem.at[0],
+                recv_sem=recv_sem.at[slot],
+                device_id={"tile": me},
+            ).wait_recv()
+
+    each_send(finish)
+
+
 def decode_kernel(
-    scal, z_ref, w1_ref, g1_ref, wm_hbm, g2_ref, hw_ref, out_ref,
-    wm, act, firstb, fscr, acc, outw, sem,
+    sizes, clip, got_ref, w1_ref, g1_ref, wm_hbm, g2_ref, hw_ref, out_ref,
+    wm, act, firstb, fscr, acc, outw, w1, rowtap, z_ref, sem,
 ):
-    hl = z_ref.shape[2]
+    tiles, strips, hl, clat, shard_rows = sizes
     ch = g1_ref.shape[-1]
-    strips = scal[7]
-    strip = scal[6]
-    patch = hw_ref.shape[-1] // 3
+    patch = hw_ref.shape[0] // 3
     half = patch // 2
     aw = WS + 3
     ow = WS + 1
     lanes = WS * half
+    rotated = (lax.axis_index("tile") + tiles - (strips // 2 - 1)) % tiles
+    strip = rotated % strips
+    block = rotated // strips
+    scal = []
+    for i in range(3 * TF):
+        at = block * TF - 2 * TF + i
+        scal.append(jnp.where(at < 0, -1, clip[jnp.maximum(at, 0)]))
+    g1 = g1_ref[...].reshape(1, ch)
+    g2 = g2_ref[...].reshape(1, ch)
 
     def tap_copies(dt):
         return [
@@ -52,6 +149,53 @@
         for copy in tap_copies(dt):
             copy.start()
 
+    group = 3 * clat
+    w1[...] = jnp.zeros_like(w1)
+    for dt in range(3):
+        for dr in range(3):
+            w1[dt, dr * GAP : dr * GAP + group] = w1_ref[dt, dr * group : (dr + 1) * group]
+    wide = rowtap.shape[0] // (hl + 2)
+    rowtap[:wide] = jnp.zeros((wide, LANES), jnp.float32)
+    rowtap[(hl + 1) * wide :] = jnp.zeros((wide, LANES), jnp.float32)
+    at_lane = lax.broadcasted_iota(jnp.int32, (wide, LANES), 1)
+    quarters = hl // shard_rows
+    per = LANES // clat
+
+    for f in range(3 * TF):
+
+        @pl.when(block * TF - 2 * TF + f < 0)
+        def _(f=f):
+            z_ref[f] = jnp.zeros(z_ref.shape[1:], jnp.bfloat16)
+
+        @pl.when(block * TF - 2 * TF + f >= 0)
+        def _(f=f):
+            @pl.loop(0, quarters)
+            def _(q):
+                piece = got_ref[f * quarters + q].astype(jnp.float32)
+                tail = piece[2 * WS :]
+                tail = jnp.concatenate([tail, pltpu.roll(tail, LANES // 2, 1)])
+                for first_row, count, x in ((0, per, piece[: 2 * WS]), (per, shard_rows - per, tail)):
+                    shifts = [x[:wide]] + [
+                        pltpu.roll(x, 2 * WS - dc, 0)[:wide] for dc in (1, 2)
+                    ]
+                    for r in range(count):
+                        y = jnp.zeros((wide, LANES), jnp.float32)
+                        for dc in (2, 1, 0):
+                            turn = (dc - r) * clat % LANES
+                            moved = pltpu.roll(shifts[dc], turn, 1) if turn else shifts[dc]
+                            y = jnp.where(at_lane < (dc + 1) * clat, moved, y)
+                        start = (1 + q * shard_rows + first_row + r) * wide
+                        rowtap[pl.ds(pl.multiple_of(start, 8), wide)] = y
+
+            @pl.loop(0, aw)
+            def _(w):
+                v = [
+                    rowtap[pl.ds(dr * wide + 8 - 3 + w, hl, stride=wide), :] for dr in range(3)
+                ]
+                low = v[0] + pltpu.roll(v[1], GAP, 1)
+                z_ref[f, w, :, :LANES] = low.astype(jnp.bfloat16)
+                z_ref[f, w, :, LANES:] = v[2].astype(jnp.bfloat16)
+
     for f in range(TF + 2):
         if f == 0:
             needed = scal[2] == scal[4]
@@ -68,7 +212,7 @@
                 lhs = z_ref[f + dt].reshape(aw * hl, z_ref.shape[-1])
                 if dt < 2:
                     lhs = lhs * keep.astype(jnp.bfloat16)
-                part = jnp.dot(lhs, w1_ref[dt], preferred_element_type=jnp.float32)
+                part = jnp.dot(lhs, w1[dt], preferred_element_type=jnp.float32)
                 total = part if total is None else total + part
             fscr[...] = total.reshape(aw, hl, ch)
 
@@ -77,7 +221,7 @@
                 rounded = fscr[w].astype(jnp.bfloat16)
                 if f >= 2:
                     firstb[f - 2, w] = rounded
-                value = norm_act(rounded.astype(jnp.float32), g1_ref[...])
+                value = norm_act(rounded.astype(jnp.float32), g1)
                 col = strip * WS + w - 2
                 inside = jnp.logical_and(col >= 0, col < strips * WS).astype(jnp.float32)
                 act[f, w] = (value * inside).astype(jnp.bfloat16)
@@ -98,7 +242,9 @@
                 acc[fo] = unit()
             else:
 
-                @pl.when(scal[fo + dt + 2] == scal[fo + 4])
+                keep = [(scal[at + dt + 2] == scal[at + 4]).astype(jnp.int32) for at in range(TF)]
+
+                @pl.when(jnp.where(fo == 0, keep[0], keep[1]) == 1)
                 def _():
                     acc[fo] += unit()
 
@@ -108,7 +254,9 @@
     colour = (cols // lanes) % 3
     want = colour * patch + (cols % lanes + half * odd) % patch
     spread = (rows == want).astype(jnp.bfloat16)
-    head = jnp.dot(hw_ref[...], spread, preferred_element_type=jnp.float32).astype(jnp.bfloat16)
+    head = lax.dot_general(
+        hw_ref[...], spread, (((0,), (0,)), ((), ())), preferred_element_type=jnp.float32
+    ).astype(jnp.bfloat16)
     lane = lax.broadcasted_iota(jnp.int32, (hl, lanes), 1)
 
     for fo in range(TF):
@@ -123,7 +271,7 @@
                 + part[:, ch : 2 * ch]
                 + row_shift(part[:, 2 * ch :], -1)
             )
-            value = norm_act(summed, g2_ref[...])
+            value = norm_act(summed, g2)
             inside = jnp.logical_or(strip > 0, w > 0).astype(jnp.float32)
             outw[fo, w % 2, w // 2] = (value * inside).astype(jnp.bfloat16)
 
@@ -147,7 +295,6 @@
 
 
 def per_device(latents, clip_index, first_conv, first_gain, middle_conv, head_gain, head_weight):
-    place = lax.axis_index("tile")
     tiles = lax.axis_size("tile")
     shard_rows, clat, wl = latents.shape
     ch = first_gain.shape[0]
@@ -155,28 +302,27 @@
     hl = tiles * shard_rows // frames
     strips = wl // WS
     half = head_weight.shape[1] // 6
-    offset = strips // 2 - 1
-    rotated = (place - offset) % tiles
-    strip = rotated % strips
-    block = rotated // strips
-
-    full = lax.all_gather(latents, "tile", axis=0, tiled=True)
-    full = full.reshape(frames, hl, clat, wl)
-    full = jnp.pad(full, ((4, 0), (0, 0), (0, 0), (3, WS + 5)))
     aw = WS + 3
-    win = lax.dynamic_slice(
-        full, (block * TF, 0, 0, strip * WS), (TF + 4, hl, clat, WS + 5)
-    ).transpose(0, 3, 1, 2)
-    win = jnp.pad(win, ((0, 0), (0, 0), (1, 1), (0, 0)))
-    z = jnp.concatenate(
-        [win[:, dc : dc + aw, dr : dr + hl] for dr in range(3) for dc in range(3)], axis=-1
-    )
-    ids = jnp.concatenate([jnp.full((4,), -1, jnp.int32), clip_index])
-    ids = lax.dynamic_slice_in_dim(ids, block * TF, TF + 4)
-    scal = jnp.concatenate([ids, jnp.stack([strip, jnp.int32(strips)]).astype(jnp.int32)])
+    quarters = tiles // frames
+    slots = 3 * TF * quarters
+    got = pl.pallas_call(
+        functools.partial(exchange_kernel, (tiles, strips, frames, shard_rows)),
+        out_shape=jax.ShapeDtypeStruct((slots, 3 * WS, LANES), jnp.bfloat16),
+        in_specs=[pl.BlockSpec(memory_space=pltpu.VMEM)],
+        out_specs=pl.BlockSpec(memory_space=pl.ANY),
+        scratch_shapes=[
+            pltpu.VMEM((8 + wl + WS, LANES), jnp.float32),
+            pltpu.VMEM((8 + wl + WS, LANES), jnp.float32),
+            pltpu.VMEM((strips, 3 * WS, LANES), jnp.bfloat16),
+            pltpu.SemaphoreType.DMA((3 * strips,)),
+            pltpu.SemaphoreType.DMA((slots,)),
+            pltpu.SemaphoreType.DMA,
+        ],
+        compiler_params=pltpu.CompilerParams(collective_id=0, has_side_effects=True),
+    )(latents.reshape(shard_rows * clat, wl))
     vm = pl.BlockSpec(memory_space=pltpu.VMEM)
     out = pl.pallas_call(
-        decode_kernel,
+        functools.partial(decode_kernel, (tiles, strips, hl, clat, shard_rows)),
         out_shape=jax.ShapeDtypeStruct((TF, 3, hl, WS * half), jnp.float32),
         in_specs=[
             pl.BlockSpec(memory_space=pltpu.SMEM), vm, vm, vm,
@@ -190,12 +336,15 @@
             pltpu.VMEM((aw, hl, ch), jnp.float32),
             pltpu.VMEM((TF, (WS + 1) * hl, 3 * ch), jnp.float32),
             pltpu.VMEM((TF, 2, WS // 2 + 1, hl, ch), jnp.bfloat16),
+            pltpu.VMEM((3, 2 * LANES, ch), jnp.bfloat16),
+            pltpu.VMEM(((hl + 2) * 24, LANES), jnp.float32),
+            pltpu.VMEM((3 * TF, aw, hl, 2 * LANES), jnp.bfloat16),
             pltpu.SemaphoreType.DMA((3,)),
         ],
         compiler_params=pltpu.CompilerParams(vmem_limit_bytes=60 * 1024 * 1024),
     )(
-        scal, z, first_conv.reshape(3, 9 * clat, ch), first_gain.reshape(1, ch), middle_conv,
-        head_gain.reshape(1, ch), head_weight,
+        clip_index, got, first_conv.reshape(3, 9 * clat, ch), first_gain, middle_conv,
+        head_gain, head_weight.T,
     )
     return out[None]
 

time: 88.2 us -> 52.9 us (0.60)
  the two profiles are of different devices: /device:TPU:3 before, /device:TPU:0 now
where the time goes in v2:
time: 52.9 us; the launch traced here: 52.6 us
  Pallas kernels  52.6 us (99%)
    pallas_call x1, Pallas kernels, per_device(): pl.pallas_call(functools.partial(decode_kernel, (tiles, strips, hl, clat,...  40.9 us
    pallas_call x1, Pallas kernels, per_device(): pl.pallas_call(functools.partial(exchange_kernel, (tiles, strips, frames,...  11.8 us

profile of v2, /device:TPU:0, one launch (start us, length us, event | category | flops | bytes accessed | tf_op | source)
XLA Modules:
  0.0 52.6 jit_solution(1092869584445568221)
XLA Ops:
  0.0 11.8 %shard_map.73.got_ref = bf16[24,48,128]{2,1,0:T(8,128)(2,1)} custom-call(bf16[192,128]{1,0:T(8,128)(2,1)} %bitcast.5), custom_call_target="tpu_custom_call" | custom-call | tf_op jit(solution)/shard_map/pallas_call | solution.py:308
  11.8 40.9 %shard_map.74 = f32[2,3,48,128]{3,2,1,0:T(8,128)} custom-call(s32[4]{0:T(128)} %clip.1, bf16[24,48,128]{2,1,0:T(8,128)(2,1)} %shard_map.73.got_ref, bf16[3,144,384]{2,1,0:T(8,128)(2,1)} %bitcast.4, f32[384]{0:T(512)} %g1_ref.1, bf16[3,3,3,384,384]{4,3,2,1,0:T(8,128)(2,1)} %wm_hbm.1, f32[384]{0:T(512)} %g2_ref.1, bf16[48,384]{1,0:T(8,128)(2,1)} %bitcast.6), custom_call_target="tpu_custom_call" | custom-call | tf_op jit(solution)/shard_map/pallas_call | solution.py:324
